TPU v7x, 128 devices: a whole 4x4x4 slice. The times are simulated.
128 devices in a mesh: tm: 32 (over z, y, core), row: 4 (over x).
Axes of the slice: x: 4, y: 4, z: 4, core: 2. Of those that a mesh axis runs over, the one named last changes fastest.
Arguments:
- edge_factor: float32 [32, 512, 512], P('tm', 'row'), may hold values from -0.25 to 0.25
- mass: float32 [32, 512], P('tm', 'row'), may hold values from 0.001 to 0.01
- rhs: float32 [32, 512, 512], P('tm', None, 'row'), may hold values from -0.25 to 0.25
Outputs:
- solution: float32 [32, 512, 512], P('tm', None, 'row')
All inputs are finite; a program needn't handle non-finite values.
Results may differ from a plain program's by a relative error of at most 0.0003.
Values sent between devices are 32-bit elements; how exact they have to be, the bound alone decides.
A program may use at most 128 MiB of HBM per device.

v0:
```python
import jax
import jax.numpy as jnp
from jax import lax
from jax.sharding import PartitionSpec as P

exact_prec = lax.Precision.HIGHEST


def passed_along(block, axis, distance):
    devices = range(lax.axis_size(axis))
    route = [(i - distance, i) for i in devices if i - distance in devices]
    return lax.ppermute(block, axis, route)


def solve_lower(factor, values):
    return jax.scipy.linalg.solve_triangular(factor, values, lower=True)


def block_cholesky(matrix):
    half = matrix.shape[0] // 2
    upper_left = jnp.linalg.cholesky(matrix[:half, :half])
    lower_left = solve_lower(upper_left, matrix[:half, half:]).T
    schur_part = matrix[half:, half:] - jnp.dot(lower_left, lower_left.T, precision=exact_prec)
    lower_right = jnp.linalg.cholesky(schur_part)
    top_rows = jnp.concatenate(
        [upper_left, jnp.zeros((half, matrix.shape[0] - half), jnp.float32)], axis=1
    )
    bottom_rows = jnp.concatenate([lower_left, lower_right], axis=1)
    return jnp.concatenate([top_rows, bottom_rows], axis=0)


def factor_split(diag_part):
    full_diag = lax.all_gather(diag_part, "row", axis=1, tiled=True)
    return block_cholesky(full_diag)


def local(edge_factor, mass, rhs):
    factor_rows = edge_factor[0]
    mass_rows = mass[0]
    rhs_cols = rhs[0]
    quarter = factor_rows.shape[0]
    node_count = factor_rows.shape[1]
    blocks = lax.axis_size("tm")
    at_start = lax.axis_index("tm") == 0
    edge_cols = jnp.dot(
        lax.all_gather(factor_rows, "row", axis=0, tiled=True),
        factor_rows.T,
        precision=exact_prec,
        preferred_element_type=jnp.float32,
    )
    edge_next = passed_along(edge_cols, "tm", -1)
    offset = lax.axis_index("row") * quarter
    row_ids = lax.broadcasted_iota(jnp.int32, (node_count, quarter), 0)
    col_ids = lax.broadcasted_iota(jnp.int32, (node_count, quarter), 1) + offset
    mass_diag = jnp.where(row_ids == col_ids, mass_rows[None, :], 0.0)
    diag_part = mass_diag + edge_cols + edge_next
    low_coupling = jnp.where(at_start, 0.0, -edge_cols)
    up_coupling = -edge_next
    stride = 1
    while stride < blocks:
        factor = factor_split(diag_part)
        whitened = solve_lower(
            factor, jnp.concatenate([low_coupling, up_coupling, rhs_cols], axis=1)
        )
        stacked = jnp.stack([whitened[:, :quarter], whitened[:, quarter : 2 * quarter]])
        gram_blocks = jnp.einsum(
            "tbn,bk->tnk",
            lax.all_gather(stacked, "row", axis=2, tiled=True),
            whitened,
            precision=exact_prec,
        )
        from_below = passed_along(gram_blocks[1], "tm", stride)
        from_above = passed_along(gram_blocks[0], "tm", -stride)
        diag_part = diag_part - from_below[:, quarter : 2 * quarter] - from_above[:, :quarter]
        low_coupling = -from_below[:, :quarter]
        up_coupling = -from_above[:, quarter : 2 * quarter]
        rhs_cols = rhs_cols - from_below[:, 2 * quarter :] - from_above[:, 2 * quarter :]
        stride = stride * 2
    factor = factor_split(diag_part)
    inner = solve_lower(factor, rhs_cols)
    solution = jax.scipy.linalg.solve_triangular(factor, inner, lower=True, trans=1)
    return solution[None]


def solution(mesh):
    placed = (P("tm", "row", None), P("tm", "row"), P("tm", None, "row"))
    return jax.shard_map(
        local, mesh=mesh, in_specs=placed, out_specs=P("tm", None, "row"), check_vma=False
    )
```

profile of v0, /device:TPU:0, one launch (start us, length us, event | category | flops | bytes accessed | tf_op | source)
XLA Modules:
  0.0 1456.5 jit_solution(16818976105928106084)
XLA Ops:
  7.3 28.3 %all-gather.36.cloned.1.call-done = f32[1,512,512]{2,1,0:T(8,128)} async-done(((f32[1,128,512]{2,1,0:T(8,128)}), f32[1,512,512]{2,1,0:T(8,128)}) %all-gather.36.cloned.1.call-update) | async-done | bytes 1048592 | tf_op jit(solution)/shard_map/all_gather | solution.py:46
  43.3 28.3 %all-gather.14.cloned.1.call-done = f32[512,512]{0,1:T(8,128)} async-done(((f32[512,128]{0,1:T(8,128)}), f32[512,512]{0,1:T(8,128)}) %all-gather.14.cloned.1.call-update) | async-done | bytes 1048592 | tf_op jit(solution)/shard_map/all_gather | solution.py:33
  73.8 11.7 cholesky.550
  95.9 11.7 cholesky.567
  114.0 19.7 %custom-call.43 = f32[2,128,128]{1,2,0:T(8,128)S(1)} custom-call(f32[2,128,128]{2,1,0:T(8,128)S(1)} %get-tuple-element.86), custom_call_target="InvertDiagBlocksLowerTriangular" | custom-call | tf_op jit(solution)/shard_map/jit(_solve_triangular)/triangular_solve | solution.py:16
  135.4 11.7 cholesky.584
  157.7 11.7 cholesky.601
  180.4 39.8 %custom-call.45 = f32[4,128,128]{1,2,0:T(8,128)S(1)} custom-call(f32[4,128,128]{2,1,0:T(8,128)S(1)} %get-tuple-element.87), custom_call_target="InvertDiagBlocksLowerTriangular" | custom-call | tf_op jit(solution)/shard_map/jit(_solve_triangular)/triangular_solve | solution.py:16
  225.3 34.4 %all-gather.16.cloned.1.call-done = f32[2,512,512]{2,1,0:T(8,128)} async-done(((f32[2,512,128]{2,1,0:T(8,128)}), f32[2,512,512]{2,1,0:T(8,128)}) %all-gather.16.cloned.1.call-update) | async-done | bytes 2097168 | tf_op jit(solution)/shard_map/all_gather | solution.py:68
  272.6 35.7 %all-gather.18.cloned.1.call-done = f32[512,512]{0,1:T(8,128)} async-done(((f32[512,128]{0,1:T(8,128)}), f32[512,512]{0,1:T(8,128)}) %all-gather.18.cloned.1.call-update) | async-done | bytes 1048592 | tf_op jit(solution)/shard_map/all_gather | solution.py:33
  310.5 11.7 cholesky.618
  332.6 11.7 cholesky.635
  351.0 19.9 %custom-call.47 = f32[2,128,128]{1,2,0:T(8,128)S(1)} custom-call(f32[2,128,128]{2,1,0:T(8,128)S(1)} %get-tuple-element.88), custom_call_target="InvertDiagBlocksLowerTriangular" | custom-call | tf_op jit(solution)/shard_map/jit(_solve_triangular)/triangular_solve | solution.py:16
  372.7 11.7 cholesky.652
  394.9 11.7 cholesky.669
  417.6 39.7 %custom-call.49 = f32[4,128,128]{1,2,0:T(8,128)S(1)} custom-call(f32[4,128,128]{2,1,0:T(8,128)S(1)} %get-tuple-element.89), custom_call_target="InvertDiagBlocksLowerTriangular" | custom-call | tf_op jit(solution)/shard_map/jit(_solve_triangular)/triangular_solve | solution.py:16
  462.5 34.4 %all-gather.20.cloned.1.call-done = f32[2,512,512]{2,1,0:T(8,128)} async-done(((f32[2,512,128]{2,1,0:T(8,128)}), f32[2,512,512]{2,1,0:T(8,128)}) %all-gather.20.cloned.1.call-update) | async-done | bytes 2097168 | tf_op jit(solution)/shard_map/all_gather | solution.py:68
  506.1 14.1 collective-permute-done.3
  525.6 26.4 %all-gather.22.cloned.1.call-done = f32[512,512]{0,1:T(8,128)} async-done(((f32[512,128]{0,1:T(8,128)}), f32[512,512]{0,1:T(8,128)}) %all-gather.22.cloned.1.call-update) | async-done | bytes 1048592 | tf_op jit(solution)/shard_map/all_gather | solution.py:33
  554.2 11.7 cholesky.686
  576.2 11.7 cholesky.703
  594.7 19.9 %custom-call.51 = f32[2,128,128]{1,2,0:T(8,128)S(1)} custom-call(f32[2,128,128]{2,1,0:T(8,128)S(1)} %get-tuple-element.90), custom_call_target="InvertDiagBlocksLowerTriangular" | custom-call | tf_op jit(solution)/shard_map/jit(_solve_triangular)/triangular_solve | solution.py:16
  616.3 11.7 cholesky.720
  638.6 11.7 cholesky.737
  661.3 39.7 %custom-call.53 = f32[4,128,128]{1,2,0:T(8,128)S(1)} custom-call(f32[4,128,128]{2,1,0:T(8,128)S(1)} %get-tuple-element.91), custom_call_target="InvertDiagBlocksLowerTriangular" | custom-call | tf_op jit(solution)/shard_map/jit(_solve_triangular)/triangular_solve | solution.py:16
  706.1 34.4 %all-gather.24.cloned.1.call-done = f32[2,512,512]{2,1,0:T(8,128)} async-done(((f32[2,512,128]{2,1,0:T(8,128)}), f32[2,512,512]{2,1,0:T(8,128)}) %all-gather.24.cloned.1.call-update) | async-done | bytes 2097168 | tf_op jit(solution)/shard_map/all_gather | solution.py:68
  751.3 14.1 collective-permute-done.5
  765.3 18.8 %collective-permute-done.6 = f32[512,384]{0,1:T(8,128)S(1)} collective-permute-done((f32[512,384]{0,1:T(8,128)S(1)}, f32[512,384]{0,1:T(8,128)S(1)}, u32[]{:S(2)}, u32[]{:S(2)}) %collective-permute-start.6) | collective-permute-done | bytes 786464 | tf_op jit(solution)/shard_map/ppermute | solution.py:12
  785.4 24.6 %all-gather.26.cloned.1.call-done = f32[512,512]{0,1:T(8,128)} async-done(((f32[512,128]{0,1:T(8,128)}), f32[512,512]{0,1:T(8,128)}) %all-gather.26.cloned.1.call-update) | async-done | bytes 1048592 | tf_op jit(solution)/shard_map/all_gather | solution.py:33
  812.2 11.7 cholesky.754
  834.3 11.7 cholesky.771
  852.7 19.9 %custom-call.55 = f32[2,128,128]{1,2,0:T(8,128)S(1)} custom-call(f32[2,128,128]{2,1,0:T(8,128)S(1)} %get-tuple-element.92), custom_call_target="InvertDiagBlocksLowerTriangular" | custom-call | tf_op jit(solution)/shard_map/jit(_solve_triangular)/triangular_solve | solution.py:16
  874.4 11.7 cholesky.788
  896.7 11.7 cholesky.805
  919.4 39.7 %custom-call.57 = f32[4,128,128]{1,2,0:T(8,128)S(1)} custom-call(f32[4,128,128]{2,1,0:T(8,128)S(1)} %get-tuple-element.93), custom_call_target="InvertDiagBlocksLowerTriangular" | custom-call | tf_op jit(solution)/shard_map/jit(_solve_triangular)/triangular_solve | solution.py:16
  964.2 34.4 %all-gather.28.cloned.1.call-done = f32[2,512,512]{2,1,0:T(8,128)} async-done(((f32[2,512,128]{2,1,0:T(8,128)}), f32[2,512,512]{2,1,0:T(8,128)}) %all-gather.28.cloned.1.call-update) | async-done | bytes 2097168 | tf_op jit(solution)/shard_map/all_gather | solution.py:68
  1007.8 14.1 collective-permute-done.7
  1027.3 24.6 %all-gather.30.cloned.1.call-done = f32[512,512]{0,1:T(8,128)} async-done(((f32[512,128]{0,1:T(8,128)}), f32[512,512]{0,1:T(8,128)}) %all-gather.30.cloned.1.call-update) | async-done | bytes 1048592 | tf_op jit(solution)/shard_map/all_gather | solution.py:33
  1054.1 11.7 cholesky.822
  1076.2 11.7 cholesky.839
  1094.6 19.9 %custom-call.59 = f32[2,128,128]{1,2,0:T(8,128)S(1)} custom-call(f32[2,128,128]{2,1,0:T(8,128)S(1)} %get-tuple-element.94), custom_call_target="InvertDiagBlocksLowerTriangular" | custom-call | tf_op jit(solution)/shard_map/jit(_solve_triangular)/triangular_solve | solution.py:16
  1161.2 39.7 %custom-call.61 = f32[4,128,128]{1,2,0:T(8,128)S(1)} custom-call(f32[4,128,128]{2,1,0:T(8,128)S(1)} %get-tuple-element.95), custom_call_target="InvertDiagBlocksLowerTriangular" | custom-call | tf_op jit(solution)/shard_map/jit(_solve_triangular)/triangular_solve | solution.py:16
  1206.1 34.4 %all-gather.32.cloned.1.call-done = f32[2,512,512]{2,1,0:T(8,128)} async-done(((f32[2,512,128]{2,1,0:T(8,128)}), f32[2,512,512]{2,1,0:T(8,128)}) %all-gather.32.cloned.1.call-update) | async-done | bytes 2097168 | tf_op jit(solution)/shard_map/all_gather | solution.py:68
  1252.5 13.7 collective-permute-done.10
  1268.3 26.7 %all-gather.34.cloned.1.call-done = f32[512,512]{0,1:T(8,128)} async-done(((f32[512,128]{0,1:T(8,128)}), f32[512,512]{0,1:T(8,128)}) %all-gather.34.cloned.1.call-update) | async-done | bytes 1048592 | tf_op jit(solution)/shard_map/all_gather | solution.py:33
  1319.3 11.7 cholesky.907
  1337.5 19.9 %custom-call.63 = f32[2,128,128]{1,2,0:T(8,128)S(1)} custom-call(f32[2,128,128]{2,1,0:T(8,128)S(1)} %get-tuple-element.96), custom_call_target="InvertDiagBlocksLowerTriangular" | custom-call | tf_op jit(solution)/shard_map/jit(_solve_triangular)/triangular_solve | solution.py:16
  1404.5 39.6 %custom-call.21 = f32[4,128,128]{1,2,0:T(8,128)S(1)} custom-call(f32[4,128,128]{2,1,0:T(8,128)S(1)} %get-tuple-element.31), custom_call_target="InvertDiagBlocksLowerTriangular" | custom-call | tf_op jit(solution)/shard_map/jit(_solve_triangular)/triangular_solve | solution.py:81
  (498 shorter events, 476.1 us)
Async XLA Ops:
  6.5 36.5 %copy-start.11 = (f32[1,512,128]{2,1,0:T(8,128)S(1)}, f32[1,512,128]{2,1,0:T(8,128)}, u32[]{:S(2)}) copy-start(f32[1,512,128]{2,1,0:T(8,128)} %param.10) | copy-start | bytes 786436
  6.5 29.1 %all-gather.36.cloned.1.call-start = ((), (), s32[]{:S(2)}) async-start(), calls=%async_computation.11 | async-start | bytes 1310720 | tf_op jit(solution)/shard_map/all_gather | solution.py:46
  7.3 64.4 %all-gather.14.cloned.1.call-start = ((), (), s32[]{:S(2)}) async-start(), calls=%async_computation | async-start | bytes 1310720 | tf_op jit(solution)/shard_map/all_gather | solution.py:33
  38.0 3.4 collective-permute-start
  43.0 216.7 %all-gather.16.cloned.1.call-start = ((), (), s32[]{:S(2)}) async-start(), calls=%async_computation.1 | async-start | bytes 2621440 | tf_op jit(solution)/shard_map/all_gather | solution.py:68
  72.6 61.1 %copy-start.5 = (f32[512,512]{0,1:T(8,128)S(1)}, f32[512,512]{0,1:T(8,128)}, u32[]{:S(2)}) copy-start(f32[512,512]{0,1:T(8,128)} %all-gather.14.cloned.1.call-done) | copy-start | bytes 3145732
  225.2 83.1 %all-gather.18.cloned.1.call-start = ((), (), s32[]{:S(2)}) async-start(), calls=%async_computation.2 | async-start | bytes 1310720 | tf_op jit(solution)/shard_map/all_gather | solution.py:33
  264.0 7.3 copy-start.3
  264.1 3.2 collective-permute-start.1
  265.5 5.9 collective-permute-start.2
  272.3 224.5 %all-gather.20.cloned.1.call-start = ((), (), s32[]{:S(2)}) async-start(), calls=%async_computation.3 | async-start | bytes 2621440 | tf_op jit(solution)/shard_map/all_gather | solution.py:68
  309.3 61.6 %copy-start.6 = (f32[512,512]{0,1:T(8,128)S(1)}, f32[512,512]{0,1:T(8,128)}, u32[]{:S(2)}) copy-start(f32[512,512]{0,1:T(8,128)} %all-gather.18.cloned.1.call-done) | copy-start | bytes 3145732
  462.4 89.5 %all-gather.22.cloned.1.call-start = ((), (), s32[]{:S(2)}) async-start(), calls=%async_computation.4 | async-start | bytes 1310720 | tf_op jit(solution)/shard_map/all_gather | solution.py:33
  501.2 23.1 %copy-start = (f32[512,128]{0,1:T(8,128)S(1)}, f32[512,128]{0,1:T(8,128)}, u32[]{:S(2)}) copy-start(f32[512,128]{0,1:T(8,128)} %get-tuple-element.245) | copy-start | bytes 786436
  501.3 18.8 %collective-permute-start.3 = (f32[512,384]{0,1:T(8,128)S(1)}, f32[512,384]{0,1:T(8,128)S(1)}, u32[]{:S(2)}, u32[]{:S(2)}) collective-permute-start(f32[512,384]{0,1:T(8,128)S(1)} %get-tuple-element.243), channel_id=1, source_target_pairs={{0,8},{4,12},{8,16},{12,20},{16,24},{20,28},{24,32},{28,36},{32,40... | collective-permute-start | bytes 2359304 | tf_op jit(solution)/shard_map/ppermute | solution.py:12
  504.8 19.5 %collective-permute-start.4 = (f32[512,384]{0,1:T(8,128)S(1)}, f32[512,384]{0,1:T(8,128)S(1)}, u32[]{:S(2)}, u32[]{:S(2)}) collective-permute-start(f32[512,384]{0,1:T(8,128)S(1)} %get-tuple-element.244), channel_id=1, source_target_pairs={{8,0},{12,4},{16,8},{20,12},{24,16},{28,20},{32,24},{36,28},{40,32... | collective-permute-start | bytes 2359304 | tf_op jit(solution)/shard_map/ppermute | solution.py:12
  525.3 215.2 %all-gather.24.cloned.1.call-start = ((), (), s32[]{:S(2)}) async-start(), calls=%async_computation.5 | async-start | bytes 2621440 | tf_op jit(solution)/shard_map/all_gather | solution.py:68
  552.9 61.6 %copy-start.7 = (f32[512,512]{0,1:T(8,128)S(1)}, f32[512,512]{0,1:T(8,128)}, u32[]{:S(2)}) copy-start(f32[512,512]{0,1:T(8,128)} %all-gather.22.cloned.1.call-done) | copy-start | bytes 3145732
  706.1 103.9 %all-gather.26.cloned.1.call-start = ((), (), s32[]{:S(2)}) async-start(), calls=%async_computation.6 | async-start | bytes 1310720 | tf_op jit(solution)/shard_map/all_gather | solution.py:33
  744.8 39.3 %copy-start.1 = (f32[512,128]{0,1:T(8,128)S(1)}, f32[512,128]{0,1:T(8,128)}, u32[]{:S(2)}) copy-start(f32[512,128]{0,1:T(8,128)} %get-tuple-element.241) | copy-start | bytes 786436
  745.0 20.3 %collective-permute-start.5 = (f32[512,384]{0,1:T(8,128)S(1)}, f32[512,384]{0,1:T(8,128)S(1)}, u32[]{:S(2)}, u32[]{:S(2)}) collective-permute-start(f32[512,384]{0,1:T(8,128)S(1)} %get-tuple-element.239), channel_id=1, source_target_pairs={{0,16},{4,20},{8,24},{12,28},{16,32},{20,36},{24,40},{28,44},{32,4... | collective-permute-start | bytes 2359304 | tf_op jit(solution)/shard_map/ppermute | solution.py:12
  750.0 34.2 %collective-permute-start.6 = (f32[512,384]{0,1:T(8,128)S(1)}, f32[512,384]{0,1:T(8,128)S(1)}, u32[]{:S(2)}, u32[]{:S(2)}) collective-permute-start(f32[512,384]{0,1:T(8,128)S(1)} %get-tuple-element.240), channel_id=1, source_target_pairs={{16,0},{20,4},{24,8},{28,12},{32,16},{36,20},{40,24},{44,28},{48,3... | collective-permute-start | bytes 2359304 | tf_op jit(solution)/shard_map/ppermute | solution.py:12
  785.1 213.4 %all-gather.28.cloned.1.call-start = ((), (), s32[]{:S(2)}) async-start(), calls=%async_computation.7 | async-start | bytes 2621440 | tf_op jit(solution)/shard_map/all_gather | solution.py:68
  811.0 61.6 %copy-start.8 = (f32[512,512]{0,1:T(8,128)S(1)}, f32[512,512]{0,1:T(8,128)}, u32[]{:S(2)}) copy-start(f32[512,512]{0,1:T(8,128)} %all-gather.26.cloned.1.call-done) | copy-start | bytes 3145732
  964.1 87.8 %all-gather.30.cloned.1.call-start = ((), (), s32[]{:S(2)}) async-start(), calls=%async_computation.8 | async-start | bytes 1310720 | tf_op jit(solution)/shard_map/all_gather | solution.py:33
  1002.9 23.2 %copy-start.2 = (f32[512,128]{0,1:T(8,128)S(1)}, f32[512,128]{0,1:T(8,128)}, u32[]{:S(2)}) copy-start(f32[512,128]{0,1:T(8,128)} %get-tuple-element.237) | copy-start | bytes 786436
  1003.0 18.9 %collective-permute-start.7 = (f32[512,384]{0,1:T(8,128)S(1)}, f32[512,384]{0,1:T(8,128)S(1)}, u32[]{:S(2)}, u32[]{:S(2)}) collective-permute-start(f32[512,384]{0,1:T(8,128)S(1)} %get-tuple-element.235), channel_id=1, source_target_pairs={{0,32},{4,36},{8,40},{12,44},{16,48},{20,52},{24,56},{28,60},{32,6... | collective-permute-start | bytes 2359304 | tf_op jit(solution)/shard_map/ppermute | solution.py:12
  1006.5 19.5 %collective-permute-start.8 = (f32[512,384]{0,1:T(8,128)S(1)}, f32[512,384]{0,1:T(8,128)S(1)}, u32[]{:S(2)}, u32[]{:S(2)}) collective-permute-start(f32[512,384]{0,1:T(8,128)S(1)} %get-tuple-element.236), channel_id=1, source_target_pairs={{32,0},{36,4},{40,8},{44,12},{48,16},{52,20},{56,24},{60,28},{64,3... | collective-permute-start | bytes 2359304 | tf_op jit(solution)/shard_map/ppermute | solution.py:12
  1027.0 213.4 %all-gather.32.cloned.1.call-start = ((), (), s32[]{:S(2)}) async-start(), calls=%async_computation.9 | async-start | bytes 2621440 | tf_op jit(solution)/shard_map/all_gather | solution.py:68
  1052.9 61.6 %copy-start.9 = (f32[512,512]{0,1:T(8,128)S(1)}, f32[512,512]{0,1:T(8,128)}, u32[]{:S(2)}) copy-start(f32[512,512]{0,1:T(8,128)} %all-gather.30.cloned.1.call-done) | copy-start | bytes 3145732
  1206.0 89.0 %all-gather.34.cloned.1.call-start = ((), (), s32[]{:S(2)}) async-start(), calls=%async_computation.10 | async-start | bytes 1310720 | tf_op jit(solution)/shard_map/all_gather | solution.py:33
  1244.8 22.7 %copy-start.4 = (f32[512,128]{0,1:T(8,128)S(1)}, f32[512,128]{0,1:T(8,128)}, u32[]{:S(2)}) copy-start(f32[512,128]{0,1:T(8,128)} %get-tuple-element.233) | copy-start | bytes 786436
  1244.9 21.3 %collective-permute-start.10 = (f32[512,384]{0,1:T(8,128)S(1)}, f32[512,384]{0,1:T(8,128)S(1)}, u32[]{:S(2)}, u32[]{:S(2)}) collective-permute-start(f32[512,384]{0,1:T(8,128)S(1)} %get-tuple-element.232), channel_id=1, source_target_pairs={{64,0},{68,4},{72,8},{76,12},{80,16},{84,20},{88,24},{92,28},{96,3... | collective-permute-start | bytes 2359304 | tf_op jit(solution)/shard_map/ppermute | solution.py:12
  1246.2 21.2 %collective-permute-start.9 = (f32[512,384]{0,1:T(8,128)S(1)}, f32[512,384]{0,1:T(8,128)S(1)}, u32[]{:S(2)}, u32[]{:S(2)}) collective-permute-start(f32[512,384]{0,1:T(8,128)S(1)} %get-tuple-element.231), channel_id=1, source_target_pairs={{0,64},{4,68},{8,72},{12,76},{16,80},{20,84},{24,88},{28,92},{32,9... | collective-permute-start | bytes 2359304 | tf_op jit(solution)/shard_map/ppermute | solution.py:12
  1296.0 61.3 %copy-start.10 = (f32[512,512]{0,1:T(8,128)S(1)}, f32[512,512]{0,1:T(8,128)}, u32[]{:S(2)}) copy-start(f32[512,512]{0,1:T(8,128)} %all-gather.34.cloned.1.call-done) | copy-start | bytes 3145732
Sparse Core Ops, SparseCore 0:
  9.0 26.5 all-gather.35
  43.1 28.4 all-gather.13
  225.3 34.2 all-gather.15
  272.4 35.8 all-gather.17
  462.5 34.2 all-gather.19
  525.4 26.5 all-gather.21
  706.2 34.2 all-gather.23
  785.2 24.7 all-gather.25
  964.2 34.2 all-gather.27
  1027.2 24.6 all-gather.29
  1206.1 34.2 all-gather.31
  1268.5 26.5 all-gather.33
where the time goes:
time: 1470 us; the launch traced here: 1460 us
  other arithmetic  792 us (54%)
  waiting for transfers between devices  458 us (31%)
  local copies, waits for them, and re-layouts  82.2 us (6%)
  matrix products  63.1 us (4%)
  between operations  31.4 us (2%)
  starting transfers between devices  28.5 us (2%)
    another operation x29, other arithmetic, solve_lower(): return jax.scipy.linalg.solve_triangular(factor, values, lower=True)  319 us
    another operation x42, other arithmetic, block_cholesky(): lower_right = jnp.linalg.cholesky(schur_part)  208 us
    another operation x41, other arithmetic, block_cholesky(): upper_left = jnp.linalg.cholesky(matrix[:half, :half])  207 us
    all_gather x5, waiting for transfers between devices, local(): lax.all_gather(stacked, 'row', axis=2, tiled=True)  172 us
    all_gather x6, waiting for transfers between devices, factor_split(): full_diag = lax.all_gather(diag_part, 'row', axis=1, tiled=True)  166 us
    ppermute x11, waiting for transfers between devices, passed_along(): return lax.ppermute(block, axis, route)  90.9 us
    another operation x116, local copies, waits for them, and re-layouts, solve_lower(): return jax.scipy.linalg.solve_triangular(factor, values, lower=True)  64.6 us
    another operation x2, other arithmetic, local(): jax.scipy.linalg.solve_triangular(factor, inner, lower=True, trans=1)  39.7 us
  transfers between devices with their start and end apart: 23, of which 23 were waited for; matrix products, arithmetic and copies ran while one was open for 0% of the time, Pallas kernels for 0%

commit v1 on v0

--- a/solution.py
+++ b/solution.py
@@ -30,7 +30,9 @@
 
 
 def factor_split(diag_part):
-    full_diag = lax.all_gather(diag_part, "row", axis=1, tiled=True)
+    full_diag = jnp.concatenate(
+        lax.all_to_all(jnp.stack([diag_part] * lax.axis_size("row")), "row", 0, 0), axis=1
+    )
     return block_cholesky(full_diag)
 
 

time: 1470 us -> 1400 us (0.952)
  waiting for transfers between devices: 458 us -> 381 us
  starting transfers between devices: 28.5 us -> 51.3 us
    all_gather x6 -> x0, waiting for transfers between devices: 166 us -> none  [factor_split(): full_diag = lax.all_gather(diag_part, 'row', axis=1, tiled=True)]
    all_to_all x0 -> x6, waiting for transfers between devices: none -> 73.6 us  [factor_split(): lax.all_to_all(jnp.stack([diag_part] * lax.axis_size('row')), 'row', 0, 0)]
    all_to_all x0 -> x6, starting transfers between devices: none -> 23.4 us  [factor_split(): lax.all_to_all(jnp.stack([diag_part] * lax.axis_size('row')), 'row', 0, 0)]
    all_gather x5, waiting for transfers between devices: 172 us -> 187 us  [local(): lax.all_gather(stacked, 'row', axis=2, tiled=True)]
where the time goes in v1:
time: 1400 us; the launch traced here: 1390 us
  other arithmetic  782 us (56%)
  waiting for transfers between devices  381 us (27%)
  local copies, waits for them, and re-layouts  83.9 us (6%)
  matrix products  63.1 us (5%)
  starting transfers between devices  51.3 us (4%)
  between operations  31.5 us (2%)
    another operation x29, other arithmetic, solve_lower(): return jax.scipy.linalg.solve_triangular(factor, values, lower=True)  319 us
    another operation x42, other arithmetic, block_cholesky(): lower_right = jnp.linalg.cholesky(schur_part)  208 us
    another operation x41, other arithmetic, block_cholesky(): upper_left = jnp.linalg.cholesky(matrix[:half, :half])  207 us
    all_gather x5, waiting for transfers between devices, local(): lax.all_gather(stacked, 'row', axis=2, tiled=True)  187 us
    ppermute x11, waiting for transfers between devices, passed_along(): return lax.ppermute(block, axis, route)  91.1 us
    all_to_all x6, waiting for transfers between devices, factor_split(): lax.all_to_all(jnp.stack([diag_part] * lax.axis_size('row')), 'row', 0, 0)  73.6 us
    another operation x116, local copies, waits for them, and re-layouts, solve_lower(): return jax.scipy.linalg.solve_triangular(factor, values, lower=True)  65.2 us
    another operation x2, other arithmetic, local(): jax.scipy.linalg.solve_triangular(factor, inner, lower=True, trans=1)  39.7 us
  transfers between devices with their start and end apart: 23, of which 23 were waited for; matrix products, arithmetic and copies ran while one was open for 0% of the time, Pallas kernels for 0%

profile of v1, /device:TPU:0, one launch (start us, length us, event | category | flops | bytes accessed | tf_op | source)
XLA Modules:
  0.0 1393.0 jit_solution(1849286465798100265)
XLA Ops:
  7.3 28.3 %all-gather.18.cloned.1.call-done = f32[1,512,512]{2,1,0:T(8,128)} async-done(((f32[1,128,512]{2,1,0:T(8,128)}), f32[1,512,512]{2,1,0:T(8,128)}) %all-gather.18.cloned.1.call-update) | async-done | bytes 1048592 | tf_op jit(solution)/shard_map/all_gather | solution.py:48
  47.2 13.0 all-to-all-done
  60.5 11.7 cholesky.550
  82.6 11.7 cholesky.567
  100.7 19.7 %custom-call.43 = f32[2,128,128]{1,2,0:T(8,128)S(1)} custom-call(f32[2,128,128]{2,1,0:T(8,128)S(1)} %get-tuple-element.86), custom_call_target="InvertDiagBlocksLowerTriangular" | custom-call | tf_op jit(solution)/shard_map/jit(_solve_triangular)/triangular_solve | solution.py:16
  122.1 11.7 cholesky.584
  144.4 11.7 cholesky.601
  167.1 39.8 %custom-call.45 = f32[4,128,128]{1,2,0:T(8,128)S(1)} custom-call(f32[4,128,128]{2,1,0:T(8,128)S(1)} %get-tuple-element.87), custom_call_target="InvertDiagBlocksLowerTriangular" | custom-call | tf_op jit(solution)/shard_map/jit(_solve_triangular)/triangular_solve | solution.py:16
  212.0 38.5 %all-gather.8.cloned.1.call-done = f32[2,512,512]{2,1,0:T(8,128)} async-done(((f32[2,512,128]{2,1,0:T(8,128)}), f32[2,512,512]{2,1,0:T(8,128)}) %all-gather.8.cloned.1.call-update) | async-done | bytes 2097168 | tf_op jit(solution)/shard_map/all_gather | solution.py:70
  278.6 11.7 cholesky.618
  300.7 11.7 cholesky.635
  319.2 19.9 %custom-call.47 = f32[2,128,128]{1,2,0:T(8,128)S(1)} custom-call(f32[2,128,128]{2,1,0:T(8,128)S(1)} %get-tuple-element.88), custom_call_target="InvertDiagBlocksLowerTriangular" | custom-call | tf_op jit(solution)/shard_map/jit(_solve_triangular)/triangular_solve | solution.py:16
  340.8 11.7 cholesky.652
  363.1 11.7 cholesky.669
  385.8 39.7 %custom-call.49 = f32[4,128,128]{1,2,0:T(8,128)S(1)} custom-call(f32[4,128,128]{2,1,0:T(8,128)S(1)} %get-tuple-element.89), custom_call_target="InvertDiagBlocksLowerTriangular" | custom-call | tf_op jit(solution)/shard_map/jit(_solve_triangular)/triangular_solve | solution.py:16
  430.6 46.8 %all-gather.10.cloned.1.call-done = f32[2,512,512]{2,1,0:T(8,128)} async-done(((f32[2,512,128]{2,1,0:T(8,128)}), f32[2,512,512]{2,1,0:T(8,128)}) %all-gather.10.cloned.1.call-update) | async-done | bytes 2097168 | tf_op jit(solution)/shard_map/all_gather | solution.py:70
  486.6 14.1 %collective-permute-done.3 = f32[512,384]{0,1:T(8,128)S(1)} collective-permute-done((f32[512,384]{0,1:T(8,128)S(1)}, f32[512,384]{0,1:T(8,128)S(1)}, u32[]{:S(2)}, u32[]{:S(2)}) %collective-permute-start.3) | collective-permute-done | bytes 786464 | tf_op jit(solution)/shard_map/ppermute | solution.py:12
  510.4 12.3 all-to-all-done.2
  523.0 11.7 cholesky.686
  545.0 11.7 cholesky.703
  563.5 19.9 %custom-call.51 = f32[2,128,128]{1,2,0:T(8,128)S(1)} custom-call(f32[2,128,128]{2,1,0:T(8,128)S(1)} %get-tuple-element.90), custom_call_target="InvertDiagBlocksLowerTriangular" | custom-call | tf_op jit(solution)/shard_map/jit(_solve_triangular)/triangular_solve | solution.py:16
  585.2 11.7 cholesky.720
  607.4 11.7 cholesky.737
  630.1 39.7 %custom-call.53 = f32[4,128,128]{1,2,0:T(8,128)S(1)} custom-call(f32[4,128,128]{2,1,0:T(8,128)S(1)} %get-tuple-element.91), custom_call_target="InvertDiagBlocksLowerTriangular" | custom-call | tf_op jit(solution)/shard_map/jit(_solve_triangular)/triangular_solve | solution.py:16
  674.9 35.1 %all-gather.12.cloned.1.call-done = f32[2,512,512]{2,1,0:T(8,128)} async-done(((f32[2,512,128]{2,1,0:T(8,128)}), f32[2,512,512]{2,1,0:T(8,128)}) %all-gather.12.cloned.1.call-update) | async-done | bytes 2097168 | tf_op jit(solution)/shard_map/all_gather | solution.py:70
  720.7 14.1 %collective-permute-done.5 = f32[512,384]{0,1:T(8,128)S(1)} collective-permute-done((f32[512,384]{0,1:T(8,128)S(1)}, f32[512,384]{0,1:T(8,128)S(1)}, u32[]{:S(2)}, u32[]{:S(2)}) %collective-permute-start.5) | collective-permute-done | bytes 786464 | tf_op jit(solution)/shard_map/ppermute | solution.py:12
  734.8 18.8 %collective-permute-done.6 = f32[512,384]{0,1:T(8,128)S(1)} collective-permute-done((f32[512,384]{0,1:T(8,128)S(1)}, f32[512,384]{0,1:T(8,128)S(1)}, u32[]{:S(2)}, u32[]{:S(2)}) %collective-permute-start.6) | collective-permute-done | bytes 786464 | tf_op jit(solution)/shard_map/ppermute | solution.py:12
  759.2 12.6 all-to-all-done.3
  772.0 11.7 cholesky.754
  794.1 11.7 cholesky.771
  812.6 19.9 %custom-call.55 = f32[2,128,128]{1,2,0:T(8,128)S(1)} custom-call(f32[2,128,128]{2,1,0:T(8,128)S(1)} %get-tuple-element.92), custom_call_target="InvertDiagBlocksLowerTriangular" | custom-call | tf_op jit(solution)/shard_map/jit(_solve_triangular)/triangular_solve | solution.py:16
  834.2 11.7 cholesky.788
  856.5 11.7 cholesky.805
  879.2 39.7 %custom-call.57 = f32[4,128,128]{1,2,0:T(8,128)S(1)} custom-call(f32[4,128,128]{2,1,0:T(8,128)S(1)} %get-tuple-element.93), custom_call_target="InvertDiagBlocksLowerTriangular" | custom-call | tf_op jit(solution)/shard_map/jit(_solve_triangular)/triangular_solve | solution.py:16
  924.0 33.2 %all-gather.14.cloned.1.call-done = f32[2,512,512]{2,1,0:T(8,128)} async-done(((f32[2,512,128]{2,1,0:T(8,128)}), f32[2,512,512]{2,1,0:T(8,128)}) %all-gather.14.cloned.1.call-update) | async-done | bytes 2097168 | tf_op jit(solution)/shard_map/all_gather | solution.py:70
  966.5 14.1 %collective-permute-done.7 = f32[512,384]{0,1:T(8,128)S(1)} collective-permute-done((f32[512,384]{0,1:T(8,128)S(1)}, f32[512,384]{0,1:T(8,128)S(1)}, u32[]{:S(2)}, u32[]{:S(2)}) %collective-permute-start.7) | collective-permute-done | bytes 786464 | tf_op jit(solution)/shard_map/ppermute | solution.py:12
  990.3 12.4 all-to-all-done.4
  1002.9 11.7 cholesky.822
  1025.0 11.7 cholesky.839
  1043.5 19.9 %custom-call.59 = f32[2,128,128]{1,2,0:T(8,128)S(1)} custom-call(f32[2,128,128]{2,1,0:T(8,128)S(1)} %get-tuple-element.94), custom_call_target="InvertDiagBlocksLowerTriangular" | custom-call | tf_op jit(solution)/shard_map/jit(_solve_triangular)/triangular_solve | solution.py:16
  1065.1 11.7 cholesky.856
  1110.1 39.7 %custom-call.61 = f32[4,128,128]{1,2,0:T(8,128)S(1)} custom-call(f32[4,128,128]{2,1,0:T(8,128)S(1)} %get-tuple-element.95), custom_call_target="InvertDiagBlocksLowerTriangular" | custom-call | tf_op jit(solution)/shard_map/jit(_solve_triangular)/triangular_solve | solution.py:16
  1154.8 33.2 %all-gather.16.cloned.1.call-done = f32[2,512,512]{2,1,0:T(8,128)} async-done(((f32[2,512,128]{2,1,0:T(8,128)}), f32[2,512,512]{2,1,0:T(8,128)}) %all-gather.16.cloned.1.call-update) | async-done | bytes 2097168 | tf_op jit(solution)/shard_map/all_gather | solution.py:70
  1200.0 13.9 collective-permute-done.10
  1220.5 12.6 all-to-all-done.5
  1255.3 11.7 cholesky.907
  1274.0 19.9 %custom-call.63 = f32[2,128,128]{1,2,0:T(8,128)S(1)} custom-call(f32[2,128,128]{2,1,0:T(8,128)S(1)} %get-tuple-element.96), custom_call_target="InvertDiagBlocksLowerTriangular" | custom-call | tf_op jit(solution)/shard_map/jit(_solve_triangular)/triangular_solve | solution.py:16
  1341.0 39.6 %custom-call.21 = f32[4,128,128]{1,2,0:T(8,128)S(1)} custom-call(f32[4,128,128]{2,1,0:T(8,128)S(1)} %get-tuple-element.31), custom_call_target="InvertDiagBlocksLowerTriangular" | custom-call | tf_op jit(solution)/shard_map/jit(_solve_triangular)/triangular_solve | solution.py:83
  (496 shorter events, 489.8 us)
Async XLA Ops:
  6.5 29.1 %all-gather.18.cloned.1.call-start = ((), (), s32[]{:S(2)}) async-start(), calls=%async_computation.11 | async-start | bytes 1310720 | tf_op jit(solution)/shard_map/all_gather | solution.py:48
  38.0 3.4 collective-permute-start
  41.5 5.5 copy-start.10
  43.4 16.8 %all-to-all-start = ((f32[4,512,128]{1,2,0:T(8,128)}), f32[4,512,128]{1,2,0:T(8,128)S(1)}, u32[]{:S(2)}, u32[]{:S(2)}) async-start(f32[4,512,128]{1,2,0:T(8,128)} %stack.42), calls=%async_computation | async-start | bytes 2097152 | tf_op jit(solution)/shard_map/all_to_all | solution.py:34
  46.9 203.6 %all-gather.8.cloned.1.call-start = ((), (), s32[]{:S(2)}) async-start(), calls=%async_computation.6 | async-start | bytes 2621440 | tf_op jit(solution)/shard_map/all_gather | solution.py:70
  47.1 35.1 %copy-start.6 = (f32[1,512,128]{1,2,0:T(8,128)}, f32[1,512,128]{1,2,0:T(8,128)S(1)}, u32[]{:S(2)}) copy-start(f32[1,512,128]{1,2,0:T(8,128)S(1)} %copy.10) | copy-start | bytes 786436
  254.8 7.3 copy-start.7
  255.0 3.2 collective-permute-start.1
  256.3 5.9 collective-permute-start.2
  262.4 5.3 copy-start
  263.6 14.8 %all-to-all-start.1 = ((f32[4,512,128]{1,2,0:T(8,128)}), f32[4,512,128]{1,2,0:T(8,128)S(1)}, u32[]{:S(2)}, u32[]{:S(2)}) async-start(f32[4,512,128]{1,2,0:T(8,128)} %stack.91), calls=%async_computation.1 | async-start | bytes 2097152 | tf_op jit(solution)/shard_map/all_to_all | solution.py:34
  267.5 209.9 %all-gather.10.cloned.1.call-start = ((), (), s32[]{:S(2)}) async-start(), calls=%async_computation.7 | async-start | bytes 2621440 | tf_op jit(solution)/shard_map/all_gather | solution.py:70
  481.7 23.1 %copy-start.1 = (f32[512,128]{0,1:T(8,128)S(1)}, f32[512,128]{0,1:T(8,128)}, u32[]{:S(2)}) copy-start(f32[512,128]{0,1:T(8,128)} %copy-done) | copy-start | bytes 786436
  481.8 18.8 %collective-permute-start.3 = (f32[512,384]{0,1:T(8,128)S(1)}, f32[512,384]{0,1:T(8,128)S(1)}, u32[]{:S(2)}, u32[]{:S(2)}) collective-permute-start(f32[512,384]{0,1:T(8,128)S(1)} %get-tuple-element.243), channel_id=1, source_target_pairs={{0,8},{4,12},{8,16},{12,20},{16,24},{20,28},{24,32},{28,36},{32,40... | collective-permute-start | bytes 2359304 | tf_op jit(solution)/shard_map/ppermute | solution.py:12
  485.3 19.5 %collective-permute-start.4 = (f32[512,384]{0,1:T(8,128)S(1)}, f32[512,384]{0,1:T(8,128)S(1)}, u32[]{:S(2)}, u32[]{:S(2)}) collective-permute-start(f32[512,384]{0,1:T(8,128)S(1)} %get-tuple-element.244), channel_id=1, source_target_pairs={{8,0},{12,4},{16,8},{20,12},{24,16},{28,20},{32,24},{36,28},{40,32... | collective-permute-start | bytes 2359304 | tf_op jit(solution)/shard_map/ppermute | solution.py:12
  505.1 5.3 copy-start.2
  506.2 16.5 %all-to-all-start.2 = ((f32[4,512,128]{1,2,0:T(8,128)}), f32[4,512,128]{1,2,0:T(8,128)S(1)}, u32[]{:S(2)}, u32[]{:S(2)}) async-start(f32[4,512,128]{1,2,0:T(8,128)} %stack.95), calls=%async_computation.2 | async-start | bytes 2097152 | tf_op jit(solution)/shard_map/all_to_all | solution.py:34
  510.1 199.8 %all-gather.12.cloned.1.call-start = ((), (), s32[]{:S(2)}) async-start(), calls=%async_computation.8 | async-start | bytes 2621440 | tf_op jit(solution)/shard_map/all_gather | solution.py:70
  714.3 39.3 %copy-start.3 = (f32[512,128]{0,1:T(8,128)S(1)}, f32[512,128]{0,1:T(8,128)}, u32[]{:S(2)}) copy-start(f32[512,128]{0,1:T(8,128)} %copy-done.2) | copy-start | bytes 786436
  714.5 20.3 %collective-permute-start.5 = (f32[512,384]{0,1:T(8,128)S(1)}, f32[512,384]{0,1:T(8,128)S(1)}, u32[]{:S(2)}, u32[]{:S(2)}) collective-permute-start(f32[512,384]{0,1:T(8,128)S(1)} %get-tuple-element.239), channel_id=1, source_target_pairs={{0,16},{4,20},{8,24},{12,28},{16,32},{20,36},{24,40},{28,44},{32,4... | collective-permute-start | bytes 2359304 | tf_op jit(solution)/shard_map/ppermute | solution.py:12
  719.4 34.2 %collective-permute-start.6 = (f32[512,384]{0,1:T(8,128)S(1)}, f32[512,384]{0,1:T(8,128)S(1)}, u32[]{:S(2)}, u32[]{:S(2)}) collective-permute-start(f32[512,384]{0,1:T(8,128)S(1)} %get-tuple-element.240), channel_id=1, source_target_pairs={{16,0},{20,4},{24,8},{28,12},{32,16},{36,20},{40,24},{44,28},{48,3... | collective-permute-start | bytes 2359304 | tf_op jit(solution)/shard_map/ppermute | solution.py:12
  753.9 5.3 copy-start.4
  755.0 16.8 %all-to-all-start.3 = ((f32[4,512,128]{1,2,0:T(8,128)}), f32[4,512,128]{1,2,0:T(8,128)S(1)}, u32[]{:S(2)}, u32[]{:S(2)}) async-start(f32[4,512,128]{1,2,0:T(8,128)} %stack.99), calls=%async_computation.3 | async-start | bytes 2097152 | tf_op jit(solution)/shard_map/all_to_all | solution.py:34
  758.9 198.3 %all-gather.14.cloned.1.call-start = ((), (), s32[]{:S(2)}) async-start(), calls=%async_computation.9 | async-start | bytes 2621440 | tf_op jit(solution)/shard_map/all_gather | solution.py:70
  961.6 23.2 %copy-start.5 = (f32[512,128]{0,1:T(8,128)S(1)}, f32[512,128]{0,1:T(8,128)}, u32[]{:S(2)}) copy-start(f32[512,128]{0,1:T(8,128)} %copy-done.4) | copy-start | bytes 786436
  961.7 18.9 %collective-permute-start.7 = (f32[512,384]{0,1:T(8,128)S(1)}, f32[512,384]{0,1:T(8,128)S(1)}, u32[]{:S(2)}, u32[]{:S(2)}) collective-permute-start(f32[512,384]{0,1:T(8,128)S(1)} %get-tuple-element.235), channel_id=1, source_target_pairs={{0,32},{4,36},{8,40},{12,44},{16,48},{20,52},{24,56},{28,60},{32,6... | collective-permute-start | bytes 2359304 | tf_op jit(solution)/shard_map/ppermute | solution.py:12
  965.2 19.5 %collective-permute-start.8 = (f32[512,384]{0,1:T(8,128)S(1)}, f32[512,384]{0,1:T(8,128)S(1)}, u32[]{:S(2)}, u32[]{:S(2)}) collective-permute-start(f32[512,384]{0,1:T(8,128)S(1)} %get-tuple-element.236), channel_id=1, source_target_pairs={{32,0},{36,4},{40,8},{44,12},{48,16},{52,20},{56,24},{60,28},{64,3... | collective-permute-start | bytes 2359304 | tf_op jit(solution)/shard_map/ppermute | solution.py:12
  985.0 5.3 copy-start.8
  986.1 16.5 %all-to-all-start.4 = ((f32[4,512,128]{1,2,0:T(8,128)}), f32[4,512,128]{1,2,0:T(8,128)S(1)}, u32[]{:S(2)}, u32[]{:S(2)}) async-start(f32[4,512,128]{1,2,0:T(8,128)} %stack.103), calls=%async_computation.4 | async-start | bytes 2097152 | tf_op jit(solution)/shard_map/all_to_all | solution.py:34
  990.1 198.0 %all-gather.16.cloned.1.call-start = ((), (), s32[]{:S(2)}) async-start(), calls=%async_computation.10 | async-start | bytes 2621440 | tf_op jit(solution)/shard_map/all_gather | solution.py:70
  1192.4 22.7 %copy-start.9 = (f32[512,128]{0,1:T(8,128)S(1)}, f32[512,128]{0,1:T(8,128)}, u32[]{:S(2)}) copy-start(f32[512,128]{0,1:T(8,128)} %copy-done.8) | copy-start | bytes 786436
  1192.5 21.3 %collective-permute-start.10 = (f32[512,384]{0,1:T(8,128)S(1)}, f32[512,384]{0,1:T(8,128)S(1)}, u32[]{:S(2)}, u32[]{:S(2)}) collective-permute-start(f32[512,384]{0,1:T(8,128)S(1)} %get-tuple-element.232), channel_id=1, source_target_pairs={{64,0},{68,4},{72,8},{76,12},{80,16},{84,20},{88,24},{92,28},{96,3... | collective-permute-start | bytes 2359304 | tf_op jit(solution)/shard_map/ppermute | solution.py:12
  1193.8 21.2 %collective-permute-start.9 = (f32[512,384]{0,1:T(8,128)S(1)}, f32[512,384]{0,1:T(8,128)S(1)}, u32[]{:S(2)}, u32[]{:S(2)}) collective-permute-start(f32[512,384]{0,1:T(8,128)S(1)} %get-tuple-element.231), channel_id=1, source_target_pairs={{0,64},{4,68},{8,72},{12,76},{16,80},{20,84},{24,88},{28,92},{32,9... | collective-permute-start | bytes 2359304 | tf_op jit(solution)/shard_map/ppermute | solution.py:12
  1216.4 16.7 %all-to-all-start.5 = ((f32[4,512,128]{1,2,0:T(8,128)}), f32[4,512,128]{1,2,0:T(8,128)S(1)}, u32[]{:S(2)}, u32[]{:S(2)}) async-start(f32[4,512,128]{1,2,0:T(8,128)} %stack.107), calls=%async_computation.5 | async-start | bytes 2097152 | tf_op jit(solution)/shard_map/all_to_all | solution.py:34
Sparse Core Ops, SparseCore 0:
  9.0 26.5 all-gather.17
  212.1 38.3 all-gather.7
  430.7 46.6 all-gather.9
  675.0 34.9 all-gather.11
  924.1 33.0 all-gather.13
  1155.0 33.0 all-gather.15
